TPU v7x, 256 devices: a whole 4x4x8 slice. The times are simulated.
256 devices in a mesh: seg: 8 (over x_hi, y), elem: 32 (over x_lo, z, core).
Axes of the slice: x: 4 (x_hi: 2, x_lo: 2; x = x_hi * 2 + x_lo), y: 4, z: 8, core: 2. Of those that a mesh axis runs over, the one named last changes fastest.
Arguments:
- base_flow: float32 [8, 3, 64, 8192], P('seg', None, None, 'elem'), may hold values from -3 to 3
- probe_field: float32 [8, 3, 64, 8192], P('seg', None, None, 'elem'), may hold values from -6 to 6
- neighbours: int32 [6, 8192], P(None, 'elem'), may hold values from 0 to 8191, as said below
- face_codes: int32 [6, 8192], P(None, 'elem'), may hold values from 0 to 23, as said below
- face_counts: int32 [8192], P('elem'), may hold values from 2 to 6
Outputs:
- first_image: float32 [8, 3, 64, 8192], P('seg', None, None, 'elem')
- second_image: float32 [8, 3, 64, 8192], P('seg', None, None, 'elem')
Inputs may be any that keep to these rules, and one draw needn't show every extreme that they name: `neighbours`: every element's neighbour in every slot, used or not, lies within 64 places of the element's own index, counted cyclically over 8192. `face_codes`: each code is 4 times a face number plus a rotation; slots past an element's count hold leftover entries.
All inputs are finite; a program needn't handle non-finite values.
Results may differ from a plain program's by a relative error of at most 0.0001.
Values sent between devices are 32-bit elements; how exact they have to be, the bound alone decides.
A program may use at most 128 MiB of HBM per device.

v0:
```python
import functools

import jax
import jax.numpy as jnp
import ml_dtypes
import numpy as np
from jax import lax
from jax.experimental import pallas as pl
from jax.experimental.pallas import tpu as pltpu
from jax.sharding import PartitionSpec as P

STEPS = 2
VISCOSITY = 0.05
PENALTY = 1.0
TIME_STEP = 0.05

COMP = 3
NODES = 64
SHARD = 256
LANES = 128
HALO = 64
EDGE = 2
SLOTS = 6


def operator_tables():
    points = np.array([-1.0, -1.0 / np.sqrt(5.0), 1.0 / np.sqrt(5.0), 1.0])
    barycentric = np.array(
        [
            1.0 / np.prod([points[row] - points[col] for col in range(4) if col != row])
            for row in range(4)
        ]
    )
    derivative = np.zeros((4, 4))
    for row in range(4):
        for col in range(4):
            if row != col:
                derivative[row, col] = (
                    barycentric[col] / barycentric[row] / (points[row] - points[col])
                )
        derivative[row, row] = -np.sum(derivative[row])
    identity = np.eye(4)
    gradient = [
        np.kron(np.kron(derivative, identity), identity),
        np.kron(np.kron(identity, derivative), identity),
        np.kron(np.kron(identity, identity), derivative),
    ]
    laplacian = sum(table @ table for table in gradient)
    return gradient, laplacian


def operator_pieces():
    gradient, laplacian = operator_tables()
    stacked = np.concatenate([VISCOSITY * laplacian] + gradient, axis=0)
    high = stacked.astype(ml_dtypes.bfloat16)
    low = (stacked - high.astype(np.float64)).astype(ml_dtypes.bfloat16)
    return jnp.asarray(np.concatenate([high, high, low, low], axis=1))


def split(value):
    high = value.astype(jnp.bfloat16)
    low = (value - high.astype(jnp.float32)).astype(jnp.bfloat16)
    return high, low


def dot(left, right):
    return jnp.dot(left, right, preferred_element_type=jnp.float32)


def kernel(
    segs,
    elems,
    base_in,
    probe_in,
    near_in,
    code_in,
    count_in,
    oper_in,
    first_ref,
    second_ref,
    oper_ref,
    near_ref,
    code_ref,
    count_ref,
    near_far,
    code_far,
    count_far,
    base,
    base_pack,
    base_far,
    state,
    acc,
    base_grad,
    own_count,
    places,
    targets,
    table,
    edge_table,
    sources,
    edge_sources,
    halo,
    follow,
    input_sem,
    list_send,
    list_recv,
    base_send,
    base_recv,
    halo_send,
    halo_recv,
    follow_send,
    follow_recv,
):
    seg = lax.axis_index("seg")
    elem = lax.axis_index("elem")
    right = lax.rem(elem + 1, elems)
    left = lax.rem(elem + elems - 1, elems)
    ahead = lax.rem(seg + 1, segs)
    behind = lax.rem(seg + segs - 1, segs)
    barrier = pltpu.get_barrier_semaphore()
    for target in ({"elem": left}, {"elem": right}, {"seg": ahead}):
        pl.semaphore_signal(
            barrier, inc=1, device_id=target, device_id_type=pl.DeviceIdType.MESH
        )
    block_lanes = (slice(0, LANES), slice(LANES, SHARD))
    pairs = [(near_in, near_ref), (code_in, code_ref), (count_in, count_ref)]
    for block in range(2):
        pairs.append((probe_in.at[:, :, block_lanes[block]], state.at[block]))
    for block in range(2):
        pairs.append((base_in.at[:, :, block_lanes[block]], base.at[block]))
    pairs.append((oper_in, oper_ref))
    loads = [
        pltpu.make_async_copy(source, target, input_sem.at[index])
        for index, (source, target) in enumerate(pairs)
    ]
    for load in loads:
        load.start()

    def across(source, target, send, recv, block):
        return pltpu.make_async_remote_copy(
            src_ref=source,
            dst_ref=target.at[1 - block],
            send_sem=send.at[block],
            recv_sem=recv.at[1 - block],
            device_id={"elem": (left, right)[block]},
            device_id_type=pl.DeviceIdType.MESH,
        )

    def list_copy(index, block):
        source, target = (
            (near_in, near_far),
            (code_in, code_far),
            (count_in, count_far),
        )[index]
        source = source.at[:, block_lanes[block]]
        return across(source, target, list_send.at[index], list_recv.at[index], block)

    def base_copy(block):
        return across(base_pack.at[block], base_far, base_send, base_recv, block)

    def halo_copy(image, block):
        source = (probe_in, first_ref)[image].at[:, :, block_lanes[block]]
        return across(source, halo.at[image], halo_send.at[image], halo_recv.at[image], block)

    def follow_copy(image):
        return arrival(image, (probe_in, first_ref)[image])

    def arrival(image, source=first_ref):
        return pltpu.make_async_remote_copy(
            src_ref=source,
            dst_ref=follow.at[image],
            send_sem=follow_send.at[image],
            recv_sem=follow_recv.at[image],
            device_id={"seg": behind},
            device_id_type=pl.DeviceIdType.MESH,
        )

    pl.semaphore_wait(barrier, 3)
    for index in range(3):
        for block in range(2):
            list_copy(index, block).start()
    for block in range(2):
        halo_copy(0, block).start()

    lane_low = lax.broadcasted_iota(jnp.int32, (NODES, LANES), 1) < HALO
    pack_low = lax.broadcasted_iota(jnp.int32, (96, LANES), 1) < HALO
    list_low = lax.broadcasted_iota(jnp.int32, (SLOTS, LANES), 1) < HALO
    row = lax.broadcasted_iota(jnp.int32, (LANES, LANES), 0)
    slot = lax.broadcasted_iota(jnp.int32, (SLOTS, LANES), 0)
    node = lax.broadcasted_iota(jnp.int32, (NODES, LANES), 0)
    node_at = (
        jnp.right_shift(node, 4),
        jnp.bitwise_and(jnp.right_shift(node, 2), 3),
        jnp.bitwise_and(node, 3),
    )
    trace = lax.broadcasted_iota(jnp.int32, (16, LANES), 0)
    trace_i, trace_j = jnp.right_shift(trace, 2), jnp.bitwise_and(trace, 3)
    blocks = elems * (SHARD // LANES)
    first_block = elem * (SHARD // LANES)

    def one_hot(chosen):
        return jnp.where(row == chosen, 1.0, 0.0).astype(jnp.bfloat16)

    def index_nodes(block, code, live):
        total = jnp.zeros((NODES, LANES), jnp.float32)
        for k in range(SLOTS):
            at = code[k : k + 1]
            way = jnp.right_shift(at, 3)
            end = 3 * jnp.bitwise_and(jnp.right_shift(at, 2), 1)
            turn = jnp.bitwise_and(at, 3)
            far = 3 - end
            place = jnp.where(
                way == 0,
                16 * far + 4 * trace_i + trace_j,
                jnp.where(
                    way == 1,
                    16 * trace_i + 4 * far + trace_j,
                    16 * trace_i + 4 * trace_j + far,
                ),
            )
            places[block, k] = place
            along = jnp.where(way == 0, node_at[0], jnp.where(way == 1, node_at[1], node_at[2]))
            i = jnp.where(way == 0, node_at[1], node_at[0])
            j = jnp.where(way == 2, node_at[1], node_at[2])
            odd = jnp.bitwise_and(turn, 1) == 1
            turned_i, turned_j = jnp.where(odd, j, i), jnp.where(odd, i, j)
            turned_i = jnp.where(turn >= 2, 3 - turned_i, turned_i)
            flip = jnp.logical_or(turn == 1, turn == 2)
            turned_j = jnp.where(flip, 3 - turned_j, turned_j)
            wanted = jnp.where(live[k : k + 1] == 1, end, -1)
            member = along == wanted
            targets[block, k] = jnp.where(member, 4 * turned_i + turned_j, 16)
            total = total + jnp.where(member, 1.0, 0.0)
        own_count[block] = total

    for load in loads[0:3]:
        load.wait()

    def own_lists(block):
        lanes = block_lanes[block]
        near = near_ref[:, lanes]
        used = slot < count_ref[:, lanes]
        place = jnp.where(used, jnp.bitwise_and(near, LANES - 1), -1)
        is_own = jnp.right_shift(near, 7) == first_block + block
        inside, beyond = jnp.where(is_own, place, -1), jnp.where(is_own, -1, place)
        for k in range(SLOTS):
            columns = slice((k % 2) * LANES, (k % 2 + 1) * LANES)
            table[block, k // 2, 0:LANES, columns] = one_hot(inside[k : k + 1])
            table[block, k // 2, LANES:SHARD, columns] = one_hot(beyond[k : k + 1])
        index_nodes(block, code_ref[:, lanes], jnp.where(used, 1, 0))

    def edge_lists():
        near = jnp.where(list_low, near_far[1], near_far[0])
        code = jnp.where(list_low, code_far[1], code_far[0])
        used = slot < jnp.where(list_low[0:1], count_far[1], count_far[0])
        place = jnp.where(used, jnp.bitwise_and(near, LANES - 1), -1)
        outer = jnp.where(
            list_low, lax.rem(first_block + 2, blocks), lax.rem(first_block + blocks - 1, blocks)
        )
        is_outer = jnp.right_shift(near, 7) == outer
        inside, beyond = jnp.where(is_outer, -1, place), jnp.where(is_outer, place, -1)
        to_left, to_right = jnp.where(list_low, -1, beyond), jnp.where(list_low, beyond, -1)
        for k in range(SLOTS):
            columns = slice((k % 2) * LANES, (k % 2 + 1) * LANES)
            for part, chosen in enumerate((inside, to_left, to_right)):
                rows = slice(part * LANES, (part + 1) * LANES)
                edge_table[k // 2, rows, columns] = one_hot(chosen[k : k + 1])
        index_nodes(EDGE, code, jnp.where(used, 1, 0))

    for load in loads[5:7]:
        load.wait()
    for block in range(2):
        packed = base[block].reshape(COMP * NODES, LANES)
        upper, lower = packed[0:96], pltpu.roll(packed[96:192], HALO, 1)
        base_pack[block] = (
            jnp.where(pack_low, upper, lower) if block == 0 else jnp.where(pack_low, lower, upper)
        )
        base_copy(block).start()
    follow_copy(0).start()
    for block in range(2):
        own_lists(block)

    def pieces_of(fields):
        return jnp.concatenate([piece for field in fields for piece in split(field)], axis=0)

    def derivatives(pieces):
        width = 2 * NODES
        beside = jnp.concatenate(
            [pieces[comp * width : (comp + 1) * width] for comp in range(COMP)], axis=1
        )
        return dot(oper_ref[...], jnp.concatenate([beside, beside], axis=0))

    def base_gradient(block):
        grads = derivatives(pieces_of([base[block, comp] for comp in range(COMP)]))
        for comp in range(COMP):
            lanes = slice(comp * LANES, (comp + 1) * LANES)
            for d in range(3):
                base_grad[block, d, comp] = grads[(d + 1) * NODES : (d + 2) * NODES, lanes]

    loads[7].wait()
    for block in range(2):
        base_gradient(block)
    for load in loads[3:5]:
        load.wait()

    def local_terms(block, pieces):
        grads = derivatives(pieces)
        for comp in range(COMP):
            lanes = slice(comp * LANES, (comp + 1) * LANES)
            total = grads[0:NODES, lanes] - own_count[block] * state[block, comp]
            for d in range(3):
                total = total - base[block, d] * grads[(d + 1) * NODES : (d + 2) * NODES, lanes]
            for d in range(3):
                total = total - state[block, d] * base_grad[block, d, comp]
            acc[block, comp] = total

    def add_flux(block, fields, weights):
        for pair in range(SLOTS // 2):
            found = dot(fields, weights(pair))
            for k in (2 * pair, 2 * pair + 1):
                lanes = slice((k % 2) * LANES, (k % 2 + 1) * LANES)
                place = places[block, k]
                target = targets[block, k]
                lookups = jnp.bitwise_and(place, 7)
                origin = jnp.right_shift(place, 3)
                for comp in range(COMP):
                    at = 2 * comp * NODES
                    value = found[at : at + NODES, lanes]
                    value = value + found[at + NODES : at + 2 * NODES, lanes]
                    halves = []
                    for half, choices in enumerate(((0, 1, 2, 3, 6), (4, 5, 6, 7, 1))):
                        rows = slice(8 * half, 8 * half + 8)
                        picked = None
                        for choice in choices:
                            option = jnp.take_along_axis(
                                value[8 * choice : 8 * choice + 8], lookups[rows], axis=0
                            )
                            picked = (
                                option
                                if picked is None
                                else jnp.where(origin[rows] == choice, option, picked)
                            )
                        halves.append(picked)
                    for group in range(8):
                        rows = slice(8 * group, 8 * group + 8)
                        goal = target[rows]
                        spot = jnp.bitwise_and(goal, 7)
                        turned = jnp.where(
                            goal < 8,
                            jnp.take_along_axis(halves[0], spot, axis=0),
                            jnp.take_along_axis(halves[1], spot, axis=0),
                        )
                        acc[block, comp, rows] += jnp.where(goal < 16, turned, 0.0)

    def blend(low, high):
        return [jnp.where(lane_low, low(comp), high(comp)) for comp in range(COMP)]

    def block_field(block):
        return lambda comp: state[block, comp]

    def own_terms(block, carry):
        pieces = pieces_of([state[block, comp] for comp in range(COMP)])
        sources[block, :, 0:LANES] = pieces
        local_terms(block, pieces)
        return carry

    def own_flux(block, carry):
        add_flux(block, sources[block], lambda pair: table[block, pair])
        return carry

    def step_forward(block, carry):
        state[block] = state[block] + TIME_STEP * acc[block]
        return carry

    def one_image(image, carry):
        lax.fori_loop(0, 2, own_terms, 0)
        edge_sources[:, 0:LANES] = pieces_of(blend(block_field(0), block_field(1)))

        @pl.when(image == 0)
        def _():
            for index in range(3):
                for block in range(2):
                    list_copy(index, block).wait_recv()
            edge_lists()

        for side in range(2):
            across(
                state.at[side], halo.at[image], halo_send.at[image], halo_recv.at[image], 1 - side
            ).wait_recv()

        def halo_field(side):
            return lambda comp: halo[image, side, comp]

        sources[0, :, LANES:SHARD] = pieces_of(blend(block_field(1), halo_field(0)))
        sources[1, :, LANES:SHARD] = pieces_of(blend(halo_field(1), block_field(0)))
        for side in range(2):
            lanes = slice((side + 1) * LANES, (side + 2) * LANES)
            edge_sources[:, lanes] = pieces_of([halo[image, side, comp] for comp in range(COMP)])
        lax.fori_loop(0, 2, own_flux, 0)
        edge = blend(halo_field(1), halo_field(0))
        for comp in range(COMP):
            state[EDGE, comp] = edge[comp]

        @pl.when(image == 0)
        def _():
            for block in range(2):
                base_copy(block).wait_recv()
            kept = jnp.where(pack_low, base_far[1], base_far[0])
            other = pltpu.roll(jnp.where(pack_low, base_far[0], base_far[1]), HALO, 1)
            base[EDGE] = jnp.concatenate([kept, other], axis=0).reshape(COMP, NODES, LANES)
            base_gradient(EDGE)

        local_terms(EDGE, pieces_of(edge))
        add_flux(EDGE, edge_sources[...], lambda pair: edge_table[pair])
        lax.fori_loop(0, 3, step_forward, 0)

        lax.fori_loop(0, 2, own_terms, 0)
        sources[0, :, LANES:SHARD] = pieces_of(blend(block_field(1), block_field(EDGE)))
        sources[1, :, LANES:SHARD] = pieces_of(blend(block_field(EDGE), block_field(0)))
        lax.fori_loop(0, 2, own_flux, 0)
        arrival(image).wait_recv()
        for block in range(2):
            lanes = block_lanes[block]
            value = state[block] + TIME_STEP * acc[block] - follow[image, :, :, lanes]
            state[block] = value

            @pl.when(image == 0)
            def _():
                first_ref[:, :, lanes] = value

            @pl.when(image == 1)
            def _():
                second_ref[:, :, lanes] = value

        @pl.when(image == 0)
        def _():
            for block in range(2):
                halo_copy(1, block).start()
            follow_copy(1).start()

        return carry

    lax.fori_loop(0, 2, one_image, 0)
    for block in range(2):
        for index in range(3):
            list_copy(index, block).wait_send()
        base_copy(block).wait_send()
        for image in range(2):
            halo_copy(image, block).wait_send()
    for image in range(2):
        follow_copy(image).wait_send()


def on_device(base_flow, probe_field, neighbours, face_codes, face_counts):
    operators = operator_pieces()
    field = jax.ShapeDtypeStruct((COMP, NODES, SHARD), jnp.float32)
    vmem = pl.BlockSpec(memory_space=pltpu.VMEM)
    first_image, second_image = pl.pallas_call(
        functools.partial(kernel, lax.axis_size("seg"), lax.axis_size("elem")),
        out_shape=(field, field),
        in_specs=[pl.BlockSpec(memory_space=pltpu.HBM)] * 6,
        out_specs=(vmem, vmem),
        scratch_shapes=[
            pltpu.VMEM(operators.shape, jnp.bfloat16),
            pltpu.VMEM((SLOTS, SHARD), jnp.int32),
            pltpu.VMEM((SLOTS, SHARD), jnp.int32),
            pltpu.VMEM((1, SHARD), jnp.int32),
            pltpu.VMEM((2, SLOTS, LANES), jnp.int32),
            pltpu.VMEM((2, SLOTS, LANES), jnp.int32),
            pltpu.VMEM((2, 1, LANES), jnp.int32),
            pltpu.VMEM((3, COMP, NODES, LANES), jnp.float32),
            pltpu.VMEM((2, 96, LANES), jnp.float32),
            pltpu.VMEM((2, 96, LANES), jnp.float32),
            pltpu.VMEM((3, COMP, NODES, LANES), jnp.float32),
            pltpu.VMEM((3, COMP, NODES, LANES), jnp.float32),
            pltpu.VMEM((3, 3, COMP, NODES, LANES), jnp.float32),
            pltpu.VMEM((3, NODES, LANES), jnp.float32),
            pltpu.VMEM((3, SLOTS, 16, LANES), jnp.int32),
            pltpu.VMEM((3, SLOTS, NODES, LANES), jnp.int32),
            pltpu.VMEM((2, SLOTS // 2, SHARD, SHARD), jnp.bfloat16),
            pltpu.VMEM((SLOTS // 2, 3 * LANES, SHARD), jnp.bfloat16),
            pltpu.VMEM((2, 2 * COMP * NODES, SHARD), jnp.bfloat16),
            pltpu.VMEM((2 * COMP * NODES, 3 * LANES), jnp.bfloat16),
            pltpu.VMEM((2, 2, COMP, NODES, LANES), jnp.float32),
            pltpu.VMEM((2, COMP, NODES, SHARD), jnp.float32),
            pltpu.SemaphoreType.DMA((8,)),
            pltpu.SemaphoreType.DMA((3, 2)),
            pltpu.SemaphoreType.DMA((3, 2)),
            pltpu.SemaphoreType.DMA((2,)),
            pltpu.SemaphoreType.DMA((2,)),
            pltpu.SemaphoreType.DMA((2, 2)),
            pltpu.SemaphoreType.DMA((2, 2)),
            pltpu.SemaphoreType.DMA((2,)),
            pltpu.SemaphoreType.DMA((2,)),
        ],
        compiler_params=pltpu.CompilerParams(
            collective_id=0, has_side_effects=True, vmem_limit_bytes=40 * 1024 * 1024
        ),
        name="shooting",
    )(
        *[
            pltpu.with_memory_space_constraint(value, pltpu.HBM)
            for value in (
                base_flow[0],
                probe_field[0],
                neighbours,
                face_codes,
                face_counts.reshape(1, SHARD),
                operators,
            )
        ]
    )
    return (first_image[None], second_image[None])


def solution(mesh):
    placed = (
        P("seg", None, None, "elem"),
        P("seg", None, None, "elem"),
        P(None, "elem"),
        P(None, "elem"),
        P("elem"),
    )
    return jax.shard_map(
        on_device,
        mesh=mesh,
        in_specs=placed,
        out_specs=(P("seg", None, None, "elem"), P("seg", None, None, "elem")),
        check_vma=False,
    )
```

profile of v0, /device:TPU:24, one launch (start us, length us, event | category | flops | bytes accessed | tf_op | source)
XLA Modules:
  0.0 26.0 jit_solution(14351725407150587867)
XLA Ops:
  0.6 24.0 %shooting.1 = (f32[3,64,256]{2,1,0:T(8,128)S(1)}, f32[3,64,256]{2,1,0:T(8,128)S(1)}) custom-call(f32[3,64,256]{2,1,0:T(8,128)} %bitcast.7, f32[3,64,256]{2,1,0:T(8,128)} %bitcast.8, s32[6,256]{1,0:T(8,128)} %near_in.1, s32[6,256]{1,0:T(8,128)} %code_in.1, s32[1,256]{1,0:T(1,128)} %bitcast.9, bf16[256,256]{1,0:T(8,128)(2,1)} %constant.2.clone.oper_in), custom_call_target="tpu_custom_call" | custom-call | tf_op jit(solution)/shard_map/shooting/pallas_call | solution.py:457
  24.7 0.7 %copy.10 = f32[1,3,64,256]{3,2,1,0:T(8,128)} copy(f32[1,3,64,256]{3,2,1,0:T(8,128)S(1)} %bitcast.6) | data formatting | bytes 393216
  25.3 0.7 %copy.11 = f32[1,3,64,256]{3,2,1,0:T(8,128)} copy(f32[1,3,64,256]{3,2,1,0:T(8,128)S(1)} %bitcast.5) | data formatting | bytes 393216
where the time goes:
time: 26.2 us; the launch traced here: 26 us
  Pallas kernels  24 us (92%)
  local copies, waits for them, and re-layouts  1.36 us (5%)
  between operations  0.64 us (2%)
    pallas_call x1, Pallas kernels, on_device(): pl.pallas_call(functools.partial(kernel, lax.axis_size('seg'), lax.axis_s...  24 us
    unnamed x2, local copies, waits for them, and re-layouts  1.36 us

commit v1 on v0

v1 whole, which is shorter than its diff:
```python
import functools

import jax
import jax.numpy as jnp
import ml_dtypes
import numpy as np
from jax import lax
from jax.experimental import pallas as pl
from jax.experimental.pallas import tpu as pltpu
from jax.sharding import PartitionSpec as P

STEPS = 2
VISCOSITY = 0.05
PENALTY = 1.0
TIME_STEP = 0.05

COMP = 3
NODES = 64
SHARD = 256
LANES = 128
HALO = 64
MIDDLE, SIDES, EDGE, OUTER = 0, 1, 2, 3
SLOTS = 6


def operator_tables():
    points = np.array([-1.0, -1.0 / np.sqrt(5.0), 1.0 / np.sqrt(5.0), 1.0])
    barycentric = np.array(
        [
            1.0 / np.prod([points[row] - points[col] for col in range(4) if col != row])
            for row in range(4)
        ]
    )
    derivative = np.zeros((4, 4))
    for row in range(4):
        for col in range(4):
            if row != col:
                derivative[row, col] = (
                    barycentric[col] / barycentric[row] / (points[row] - points[col])
                )
        derivative[row, row] = -np.sum(derivative[row])
    identity = np.eye(4)
    gradient = [
        np.kron(np.kron(derivative, identity), identity),
        np.kron(np.kron(identity, derivative), identity),
        np.kron(np.kron(identity, identity), derivative),
    ]
    laplacian = sum(table @ table for table in gradient)
    return gradient, laplacian


def operator_pieces():
    gradient, laplacian = operator_tables()
    stacked = np.concatenate([VISCOSITY * laplacian] + gradient, axis=0)
    high = stacked.astype(ml_dtypes.bfloat16)
    low = (stacked - high.astype(np.float64)).astype(ml_dtypes.bfloat16)
    return jnp.asarray(np.concatenate([high, high, low, low], axis=1))


def split(value):
    high = value.astype(jnp.bfloat16)
    low = (value - high.astype(jnp.float32)).astype(jnp.bfloat16)
    return high, low


def dot(left, right):
    return jnp.dot(left, right, preferred_element_type=jnp.float32)


def kernel(
    segs,
    elems,
    base_in,
    probe_in,
    near_in,
    code_in,
    count_in,
    oper_in,
    first_ref,
    second_ref,
    oper_ref,
    near_ref,
    code_ref,
    count_ref,
    near_far,
    code_far,
    count_far,
    loaded,
    base,
    base_pack,
    base_far,
    state,
    acc,
    base_grad,
    own_count,
    places,
    turns,
    faces,
    table,
    sources,
    gathered,
    halo,
    follow,
    input_sem,
    list_send,
    list_recv,
    base_send,
    base_recv,
    halo_send,
    halo_recv,
    follow_send,
    follow_recv,
):
    seg = lax.axis_index("seg")
    elem = lax.axis_index("elem")
    right = lax.rem(elem + 1, elems)
    left = lax.rem(elem + elems - 1, elems)
    ahead = lax.rem(seg + 1, segs)
    behind = lax.rem(seg + segs - 1, segs)
    barrier = pltpu.get_barrier_semaphore()
    for target in ({"elem": left}, {"elem": right}, {"seg": ahead}):
        pl.semaphore_signal(
            barrier, inc=1, device_id=target, device_id_type=pl.DeviceIdType.MESH
        )
    block_lanes = (slice(0, LANES), slice(LANES, SHARD))
    pairs = [(near_in, near_ref), (code_in, code_ref), (count_in, count_ref)]
    for block in range(2):
        pairs.append((probe_in.at[:, :, block_lanes[block]], loaded.at[0, block]))
    for block in range(2):
        pairs.append((base_in.at[:, :, block_lanes[block]], loaded.at[1, block]))
    pairs.append((oper_in, oper_ref))
    loads = [
        pltpu.make_async_copy(source, target, input_sem.at[index])
        for index, (source, target) in enumerate(pairs)
    ]
    for load in loads:
        load.start()

    def across(source, target, send, recv, block):
        return pltpu.make_async_remote_copy(
            src_ref=source,
            dst_ref=target.at[1 - block],
            send_sem=send.at[block],
            recv_sem=recv.at[1 - block],
            device_id={"elem": (left, right)[block]},
            device_id_type=pl.DeviceIdType.MESH,
        )

    def list_copy(index, block):
        source, target = (
            (near_in, near_far),
            (code_in, code_far),
            (count_in, count_far),
        )[index]
        source = source.at[:, block_lanes[block]]
        return across(source, target, list_send.at[index], list_recv.at[index], block)

    def base_copy(block):
        return across(base_pack.at[block], base_far, base_send, base_recv, block)

    def halo_copy(image, block):
        source = (probe_in, first_ref)[image].at[:, :, block_lanes[block]]
        return across(source, halo.at[image], halo_send.at[image], halo_recv.at[image], block)

    def follow_copy(image):
        return arrival(image, (probe_in, first_ref)[image])

    def arrival(image, source=first_ref):
        return pltpu.make_async_remote_copy(
            src_ref=source,
            dst_ref=follow.at[image],
            send_sem=follow_send.at[image],
            recv_sem=follow_recv.at[image],
            device_id={"seg": behind},
            device_id_type=pl.DeviceIdType.MESH,
        )

    pl.semaphore_wait(barrier, 3)
    for index in range(3):
        for block in range(2):
            list_copy(index, block).start()
    for block in range(2):
        halo_copy(0, block).start()

    lane_low = lax.broadcasted_iota(jnp.int32, (NODES, LANES), 1) < HALO
    pack_low = lax.broadcasted_iota(jnp.int32, (96, LANES), 1) < HALO
    list_low = lax.broadcasted_iota(jnp.int32, (SLOTS, LANES), 1) < HALO
    count_low = lax.broadcasted_iota(jnp.int32, (1, LANES), 1) < HALO
    row = lax.broadcasted_iota(jnp.int32, (LANES, LANES), 0)
    slot = lax.broadcasted_iota(jnp.int32, (SLOTS, LANES), 0)
    node = lax.broadcasted_iota(jnp.int32, (NODES, LANES), 0)
    node_at = (
        jnp.right_shift(node, 4),
        jnp.bitwise_and(jnp.right_shift(node, 2), 3),
        jnp.bitwise_and(node, 3),
    )
    trace = lax.broadcasted_iota(jnp.int32, (16, LANES), 0)
    trace_i, trace_j = jnp.right_shift(trace, 2), jnp.bitwise_and(trace, 3)
    sublane = lax.broadcasted_iota(jnp.int32, (8, LANES), 0)
    blocks = elems * (SHARD // LANES)
    block_a = elem * (SHARD // LANES)
    before_a = lax.rem(block_a + blocks - 1, blocks)
    after_b = lax.rem(block_a + 2, blocks)

    def index_block(block, near, code, count):
        used = slot < count
        lane = jnp.bitwise_and(near, LANES - 1)
        origin = jnp.right_shift(near, 7)
        high = lane >= HALO
        in_a, in_b = origin == block_a, origin == block_a + 1
        back = origin == before_a
        own = jnp.logical_or(in_a, in_b)
        middle = jnp.logical_and(own, in_a == high)
        outer = jnp.logical_and(jnp.logical_not(own), back != high)
        kind = jnp.where(own, jnp.where(middle, MIDDLE, SIDES), jnp.where(outer, OUTER, EDGE))
        kind = jnp.where(used, kind, -1)
        first = 1 if block == EDGE else 0
        for part in range(2 if block == MIDDLE else 3):
            chosen = jnp.where(kind == first + part, lane, -1)
            rows = slice(part * LANES, (part + 1) * LANES)
            for k in range(SLOTS):
                columns = slice((k % 2) * LANES, (k % 2 + 1) * LANES)
                table[block, k // 2, rows, columns] = jnp.where(
                    row == chosen[k : k + 1], 1.0, 0.0
                ).astype(jnp.bfloat16)
        way = jnp.right_shift(code, 3)
        far = 3 - 3 * jnp.bitwise_and(jnp.right_shift(code, 2), 1)
        turn = jnp.bitwise_and(code, 3)
        face = jnp.right_shift(code, 2)
        total = jnp.zeros((NODES, LANES), jnp.float32)
        for which in range(6):
            hits = jnp.where(jnp.logical_and(face == which, used), 1.0, 0.0)
            on_face = node_at[which // 2] == 3 * (which % 2)
            total = total + jnp.where(on_face, jnp.sum(hits, axis=0, keepdims=True), 0.0)
        own_count[block] = total
        for k in range(SLOTS):
            row_way, row_far, row_turn = way[k : k + 1], far[k : k + 1], turn[k : k + 1]
            places[block, k] = jnp.where(
                row_way == 0,
                16 * row_far + 4 * trace_i + trace_j,
                jnp.where(
                    row_way == 1,
                    16 * trace_i + 4 * row_far + trace_j,
                    16 * trace_i + 4 * trace_j + row_far,
                ),
            )
            odd = jnp.bitwise_and(row_turn, 1) == 1
            turned_i = jnp.where(odd, trace_j, trace_i)
            turned_j = jnp.where(odd, trace_i, trace_j)
            turned_i = jnp.where(row_turn >= 2, 3 - turned_i, turned_i)
            flip = jnp.logical_or(row_turn == 1, row_turn == 2)
            turned_j = jnp.where(flip, 3 - turned_j, turned_j)
            turns[block, k] = 4 * turned_i + turned_j
            faces[block, k] = jnp.broadcast_to(face[k : k + 1], (8, LANES))

    def pieces_of(fields):
        return jnp.concatenate([piece for field in fields for piece in split(field)], axis=0)

    def derivatives(pieces):
        width = 2 * NODES
        beside = jnp.concatenate(
            [pieces[comp * width : (comp + 1) * width] for comp in range(COMP)], axis=1
        )
        return dot(oper_ref[...], jnp.concatenate([beside, beside], axis=0))

    def base_gradient(block):
        grads = derivatives(pieces_of([base[block, comp] for comp in range(COMP)]))
        for comp in range(COMP):
            lanes = slice(comp * LANES, (comp + 1) * LANES)
            for d in range(3):
                base_grad[block, d, comp] = grads[(d + 1) * NODES : (d + 2) * NODES, lanes]

    for load in loads[5:7]:
        load.wait()
    for block in range(2):
        packed = loaded[1, block].reshape(COMP * NODES, LANES)
        upper, lower = packed[0:96], pltpu.roll(packed[96:192], HALO, 1)
        base_pack[block] = (
            jnp.where(pack_low, upper, lower) if block == 0 else jnp.where(pack_low, lower, upper)
        )
        base_copy(block).start()
    follow_copy(0).start()
    for load in loads[0:5]:
        load.wait()
    for comp in range(COMP):
        for target, kind in ((state, 0), (base, 1)):
            in_a, in_b = loaded[kind, 0, comp], loaded[kind, 1, comp]
            target[MIDDLE, comp] = jnp.where(lane_low, in_b, in_a)
            target[SIDES, comp] = jnp.where(lane_low, in_a, in_b)
    for block in (MIDDLE, SIDES):
        lists = []
        for ref, low in ((near_ref, list_low), (code_ref, list_low), (count_ref, count_low)):
            in_a, in_b = ref[:, 0:LANES], ref[:, LANES:SHARD]
            if block == MIDDLE:
                in_a, in_b = in_b, in_a
            lists.append(jnp.where(low, in_a, in_b))
        index_block(block, *lists)
    loads[7].wait()
    for block in (MIDDLE, SIDES):
        base_gradient(block)

    def local_terms(block, pieces, started):
        grads = derivatives(pieces)
        for comp in range(COMP):
            lanes = slice(comp * LANES, (comp + 1) * LANES)
            total = grads[0:NODES, lanes] - own_count[block] * state[block, comp]
            for d in range(3):
                total = total - base[block, d] * grads[(d + 1) * NODES : (d + 2) * NODES, lanes]
            for d in range(3):
                total = total - state[block, d] * base_grad[block, d, comp]
            acc[block, comp] = total + acc[block, comp] if started else total

    def add_flux(block, fields, depth):
        for pair in range(SLOTS // 2):
            found = dot(fields, table[block, pair, 0:depth])
            for comp in range(COMP):
                at = 2 * comp * NODES
                value = found[at : at + NODES] + found[at + NODES : at + 2 * NODES]
                gathered[2 * pair, comp] = value[:, 0:LANES]
                gathered[2 * pair + 1, comp] = value[:, LANES:SHARD]

        def component(comp, carry):
            sums = [[None, None] for _ in range(6)]
            for k in range(SLOTS):
                halves = []
                for half, choices in enumerate(((0, 1, 2, 3, 6), (4, 5, 6, 7, 1))):
                    place = places[block, k, 8 * half : 8 * half + 8]
                    lookup = jnp.bitwise_and(place, 7)
                    origin = jnp.right_shift(place, 3)
                    picked = None
                    for choice in choices:
                        option = jnp.take_along_axis(
                            gathered[k, comp, 8 * choice : 8 * choice + 8], lookup, axis=0
                        )
                        picked = (
                            option
                            if picked is None
                            else jnp.where(origin == choice, option, picked)
                        )
                    halves.append(picked)
                for half in range(2):
                    goal = turns[block, k, 8 * half : 8 * half + 8]
                    spot = jnp.bitwise_and(goal, 7)
                    turned = jnp.where(
                        goal < 8,
                        jnp.take_along_axis(halves[0], spot, axis=0),
                        jnp.take_along_axis(halves[1], spot, axis=0),
                    )
                    for which in range(6):
                        term = jnp.where(faces[block, k] == which, turned, 0.0)
                        held = sums[which][half]
                        sums[which][half] = term if held is None else held + term
            swapped = jnp.bitwise_xor(sublane, 4)
            edge_of = jnp.bitwise_and(sublane, 3)
            for group in range(8):
                half, odd_a = group // 4, (group // 2) % 2
                rows = slice(8 * group, 8 * group + 8)
                total = acc[block, comp, rows]
                if group < 2:
                    total = total + sums[0][group]
                if group >= 6:
                    total = total + sums[1][group - 6]
                side = sums[2 + group % 2][half]
                if odd_a != group % 2:
                    side = jnp.take_along_axis(side, swapped, axis=0)
                total = total + jnp.where((sublane < 4) == (group % 2 == 0), side, 0.0)
                spot = 2 * (group % 4) + jnp.right_shift(sublane, 2)
                front = jnp.take_along_axis(sums[4][half], spot, axis=0)
                rear = jnp.take_along_axis(sums[5][half], spot, axis=0)
                total = total + jnp.where(edge_of == 0, front, jnp.where(edge_of == 3, rear, 0.0))
                acc[block, comp, rows] = total
            return carry

        lax.fori_loop(0, COMP, component, 0)

    def blend(low, high):
        return [jnp.where(lane_low, low[comp], high[comp]) for comp in range(COMP)]

    def own_terms(block, carry):
        pieces = pieces_of([state[block, comp] for comp in range(COMP)])
        sources[block] = pieces
        local_terms(block, pieces, False)
        return carry

    def wide_flux(block, carry):
        fields = jnp.concatenate([sources[block - 1 + part] for part in range(3)], axis=1)
        add_flux(block, fields, 3 * LANES)
        return carry

    def step_forward(block, carry):
        state[block] = state[block] + TIME_STEP * acc[block]
        return carry

    def one_step(step, carry):
        image, odd = step // STEPS, step % STEPS
        lax.fori_loop(MIDDLE, EDGE, own_terms, 0)
        fields = jnp.concatenate([sources[MIDDLE], sources[SIDES]], axis=1)
        add_flux(MIDDLE, fields, SHARD)

        @pl.when(step == 0)
        def _():
            for index in range(3):
                for block in range(2):
                    list_copy(index, block).wait_recv()
            index_block(
                EDGE,
                jnp.where(list_low, near_far[1], near_far[0]),
                jnp.where(list_low, code_far[1], code_far[0]),
                jnp.where(count_low, count_far[1], count_far[0]),
            )

        @pl.when(odd == 0)
        def _():
            for side in range(2):
                across(
                    loaded.at[0, side],
                    halo.at[image],
                    halo_send.at[image],
                    halo_recv.at[image],
                    1 - side,
                ).wait_recv()
            from_left = [halo[image, 0, comp] for comp in range(COMP)]
            from_right = [halo[image, 1, comp] for comp in range(COMP)]
            edge = blend(from_right, from_left)
            for comp in range(COMP):
                state[EDGE, comp] = edge[comp]
            sources[OUTER] = pieces_of(blend(from_left, from_right))
            acc[EDGE] = jnp.zeros((COMP, NODES, LANES), jnp.float32)

        sources[EDGE] = pieces_of([state[EDGE, comp] for comp in range(COMP)])
        done = EDGE + 1 - odd
        lax.fori_loop(SIDES, done, wide_flux, 0)

        @pl.when(step == 0)
        def _():
            for block in range(2):
                base_copy(block).wait_recv()
            kept = jnp.where(pack_low, base_far[1], base_far[0])
            other = pltpu.roll(jnp.where(pack_low, base_far[0], base_far[1]), HALO, 1)
            base[EDGE] = jnp.concatenate([kept, other], axis=0).reshape(COMP, NODES, LANES)
            base_gradient(EDGE)

        @pl.when(odd == 0)
        def _():
            local_terms(EDGE, sources[EDGE], True)

        lax.fori_loop(MIDDLE, done, step_forward, 0)

        @pl.when(odd == 1)
        def _():
            arrival(image).wait_recv()
            for comp in range(COMP):
                middle, sides = state[MIDDLE, comp], state[SIDES, comp]
                in_a = jnp.where(lane_low, sides, middle) - follow[image, comp, :, 0:LANES]
                in_b = jnp.where(lane_low, middle, sides) - follow[image, comp, :, LANES:SHARD]

                @pl.when(image == 0)
                def _():
                    first_ref[comp, :, 0:LANES] = in_a
                    first_ref[comp, :, LANES:SHARD] = in_b
                    state[MIDDLE, comp] = jnp.where(lane_low, in_b, in_a)
                    state[SIDES, comp] = jnp.where(lane_low, in_a, in_b)

                @pl.when(image == 1)
                def _():
                    second_ref[comp, :, 0:LANES] = in_a
                    second_ref[comp, :, LANES:SHARD] = in_b

        @pl.when(step == STEPS - 1)
        def _():
            for block in range(2):
                halo_copy(1, block).start()
            follow_copy(1).start()

        return carry

    lax.fori_loop(0, 2 * STEPS, one_step, 0)
    for block in range(2):
        for index in range(3):
            list_copy(index, block).wait_send()
        base_copy(block).wait_send()
        for image in range(2):
            halo_copy(image, block).wait_send()
    for image in range(2):
        follow_copy(image).wait_send()


def on_device(base_flow, probe_field, neighbours, face_codes, face_counts):
    operators = operator_pieces()
    field = jax.ShapeDtypeStruct((COMP, NODES, SHARD), jnp.float32)
    vmem = pl.BlockSpec(memory_space=pltpu.VMEM)
    first_image, second_image = pl.pallas_call(
        functools.partial(kernel, lax.axis_size("seg"), lax.axis_size("elem")),
        out_shape=(field, field),
        in_specs=[pl.BlockSpec(memory_space=pltpu.HBM)] * 6,
        out_specs=(vmem, vmem),
        scratch_shapes=[
            pltpu.VMEM(operators.shape, jnp.bfloat16),
            pltpu.VMEM((SLOTS, SHARD), jnp.int32),
            pltpu.VMEM((SLOTS, SHARD), jnp.int32),
            pltpu.VMEM((1, SHARD), jnp.int32),
            pltpu.VMEM((2, SLOTS, LANES), jnp.int32),
            pltpu.VMEM((2, SLOTS, LANES), jnp.int32),
            pltpu.VMEM((2, 1, LANES), jnp.int32),
            pltpu.VMEM((2, 2, COMP, NODES, LANES), jnp.float32),
            pltpu.VMEM((3, COMP, NODES, LANES), jnp.float32),
            pltpu.VMEM((2, 96, LANES), jnp.float32),
            pltpu.VMEM((2, 96, LANES), jnp.float32),
            pltpu.VMEM((3, COMP, NODES, LANES), jnp.float32),
            pltpu.VMEM((3, COMP, NODES, LANES), jnp.float32),
            pltpu.VMEM((3, 3, COMP, NODES, LANES), jnp.float32),
            pltpu.VMEM((3, NODES, LANES), jnp.float32),
            pltpu.VMEM((3, SLOTS, 16, LANES), jnp.int32),
            pltpu.VMEM((3, SLOTS, 16, LANES), jnp.int32),
            pltpu.VMEM((3, SLOTS, 8, LANES), jnp.int32),
            pltpu.VMEM((3, SLOTS // 2, 3 * LANES, SHARD), jnp.bfloat16),
            pltpu.VMEM((4, 2 * COMP * NODES, LANES), jnp.bfloat16),
            pltpu.VMEM((SLOTS, COMP, NODES, LANES), jnp.float32),
            pltpu.VMEM((2, 2, COMP, NODES, LANES), jnp.float32),
            pltpu.VMEM((2, COMP, NODES, SHARD), jnp.float32),
            pltpu.SemaphoreType.DMA((8,)),
            pltpu.SemaphoreType.DMA((3, 2)),
            pltpu.SemaphoreType.DMA((3, 2)),
            pltpu.SemaphoreType.DMA((2,)),
            pltpu.SemaphoreType.DMA((2,)),
            pltpu.SemaphoreType.DMA((2, 2)),
            pltpu.SemaphoreType.DMA((2, 2)),
            pltpu.SemaphoreType.DMA((2,)),
            pltpu.SemaphoreType.DMA((2,)),
        ],
        compiler_params=pltpu.CompilerParams(
            collective_id=0, has_side_effects=True, vmem_limit_bytes=40 * 1024 * 1024
        ),
        name="shooting",
    )(
        *[
            pltpu.with_memory_space_constraint(value, pltpu.HBM)
            for value in (
                base_flow[0],
                probe_field[0],
                neighbours,
                face_codes,
                face_counts.reshape(1, SHARD),
                operators,
            )
        ]
    )
    return (first_image[None], second_image[None])


def solution(mesh):
    placed = (
        P("seg", None, None, "elem"),
        P("seg", None, None, "elem"),
        P(None, "elem"),
        P(None, "elem"),
        P("elem"),
    )
    return jax.shard_map(
        on_device,
        mesh=mesh,
        in_specs=placed,
        out_specs=(P("seg", None, None, "elem"), P("seg", None, None, "elem")),
        check_vma=False,
    )
```

time: 26.2 us -> 26.9 us (1.027)
  Pallas kernels: 24 us -> 24.8 us
    pallas_call x1, Pallas kernels: 24 us -> 24.8 us  [on_device(): pl.pallas_call(functools.partial(kernel, lax.axis_size('seg'), lax.axis_s...]
where the time goes in v1:
time: 26.9 us; the launch traced here: 26.8 us
  Pallas kernels  24.8 us (92%)
  local copies, waits for them, and re-layouts  1.36 us (5%)
  between operations  0.64 us (2%)
    pallas_call x1, Pallas kernels, on_device(): pl.pallas_call(functools.partial(kernel, lax.axis_size('seg'), lax.axis_s...  24.8 us
    unnamed x2, local copies, waits for them, and re-layouts  1.36 us

profile of v1, /device:TPU:24, one launch (start us, length us, event | category | flops | bytes accessed | tf_op | source)
XLA Modules:
  0.0 26.8 jit_solution(13060744516015704063)
XLA Ops:
  0.6 24.8 %shooting.1 = (f32[3,64,256]{2,1,0:T(8,128)S(1)}, f32[3,64,256]{2,1,0:T(8,128)S(1)}) custom-call(f32[3,64,256]{2,1,0:T(8,128)} %bitcast.7, f32[3,64,256]{2,1,0:T(8,128)} %bitcast.8, s32[6,256]{1,0:T(8,128)} %near_in.1, s32[6,256]{1,0:T(8,128)} %code_in.1, s32[1,256]{1,0:T(1,128)} %bitcast.9, bf16[256,256]{1,0:T(8,128)(2,1)} %constant.2.clone.oper_in), custom_call_target="tpu_custom_call" | custom-call | tf_op jit(solution)/shard_map/shooting/pallas_call | solution.py:492
  25.5 0.7 %copy.10 = f32[1,3,64,256]{3,2,1,0:T(8,128)} copy(f32[1,3,64,256]{3,2,1,0:T(8,128)S(1)} %bitcast.6) | data formatting | bytes 393216
  26.2 0.7 %copy.11 = f32[1,3,64,256]{3,2,1,0:T(8,128)} copy(f32[1,3,64,256]{3,2,1,0:T(8,128)S(1)} %bitcast.5) | data formatting | bytes 393216

commit v2 on v0

--- a/solution.py
+++ b/solution.py
@@ -357,26 +357,20 @@
     def block_field(block):
         return lambda comp: state[block, comp]
 
-    def own_terms(block, carry):
+    def own_terms(block):
         pieces = pieces_of([state[block, comp] for comp in range(COMP)])
         sources[block, :, 0:LANES] = pieces
         local_terms(block, pieces)
-        return carry
-
-    def own_flux(block, carry):
+
+    def own_flux(block):
         add_flux(block, sources[block], lambda pair: table[block, pair])
-        return carry
-
-    def step_forward(block, carry):
-        state[block] = state[block] + TIME_STEP * acc[block]
-        return carry
-
-    def one_image(image, carry):
-        lax.fori_loop(0, 2, own_terms, 0)
+
+    def one_image(image):
+        for block in range(2):
+            own_terms(block)
         edge_sources[:, 0:LANES] = pieces_of(blend(block_field(0), block_field(1)))
 
-        @pl.when(image == 0)
-        def _():
+        if image == 0:
             for index in range(3):
                 for block in range(2):
                     list_copy(index, block).wait_recv()
@@ -395,13 +389,13 @@
         for side in range(2):
             lanes = slice((side + 1) * LANES, (side + 2) * LANES)
             edge_sources[:, lanes] = pieces_of([halo[image, side, comp] for comp in range(COMP)])
-        lax.fori_loop(0, 2, own_flux, 0)
+        for block in range(2):
+            own_flux(block)
         edge = blend(halo_field(1), halo_field(0))
         for comp in range(COMP):
             state[EDGE, comp] = edge[comp]
 
-        @pl.when(image == 0)
-        def _():
+        if image == 0:
             for block in range(2):
                 base_copy(block).wait_recv()
             kept = jnp.where(pack_low, base_far[1], base_far[0])
@@ -411,35 +405,28 @@
 
         local_terms(EDGE, pieces_of(edge))
         add_flux(EDGE, edge_sources[...], lambda pair: edge_table[pair])
-        lax.fori_loop(0, 3, step_forward, 0)
-
-        lax.fori_loop(0, 2, own_terms, 0)
+        for block in range(3):
+            state[block] = state[block] + TIME_STEP * acc[block]
+
+        for block in range(2):
+            own_terms(block)
         sources[0, :, LANES:SHARD] = pieces_of(blend(block_field(1), block_field(EDGE)))
         sources[1, :, LANES:SHARD] = pieces_of(blend(block_field(EDGE), block_field(0)))
-        lax.fori_loop(0, 2, own_flux, 0)
+        for block in range(2):
+            own_flux(block)
         arrival(image).wait_recv()
         for block in range(2):
             lanes = block_lanes[block]
             value = state[block] + TIME_STEP * acc[block] - follow[image, :, :, lanes]
-            state[block] = value
-
-            @pl.when(image == 0)
-            def _():
-                first_ref[:, :, lanes] = value
-
-            @pl.when(image == 1)
-            def _():
-                second_ref[:, :, lanes] = value
-
-        @pl.when(image == 0)
-        def _():
-            for block in range(2):
+            (first_ref, second_ref)[image][:, :, lanes] = value
+            if image == 0:
+                state[block] = value
                 halo_copy(1, block).start()
+        if image == 0:
             follow_copy(1).start()
 
-        return carry
-
-    lax.fori_loop(0, 2, one_image, 0)
+    for image in range(2):
+        one_image(image)
     for block in range(2):
         for index in range(3):
             list_copy(index, block).wait_send()

time: 26.2 us -> 25 us (0.954)
  Pallas kernels: 24 us -> 22.9 us
    pallas_call x1, Pallas kernels: 24 us -> 22.9 us  [on_device(): pl.pallas_call(functools.partial(kernel, lax.axis_size('seg'), lax.axis_s...]
where the time goes in v2:
time: 25 us; the launch traced here: 24.9 us
  Pallas kernels  22.9 us (92%)
  local copies, waits for them, and re-layouts  1.36 us (5%)
  between operations  0.64 us (3%)
    pallas_call x1, Pallas kernels, on_device(): pl.pallas_call(functools.partial(kernel, lax.axis_size('seg'), lax.axis_s...  22.9 us
    unnamed x2, local copies, waits for them, and re-layouts  1.36 us

profile of v2, /device:TPU:24, one launch (start us, length us, event | category | flops | bytes accessed | tf_op | source)
XLA Modules:
  0.0 24.9 jit_solution(14484925843668037687)
XLA Ops:
  0.6 22.9 %shooting.1 = (f32[3,64,256]{2,1,0:T(8,128)S(1)}, f32[3,64,256]{2,1,0:T(8,128)S(1)}) custom-call(f32[3,64,256]{2,1,0:T(8,128)} %bitcast.7, f32[3,64,256]{2,1,0:T(8,128)} %bitcast.8, s32[6,256]{1,0:T(8,128)} %near_in.1, s32[6,256]{1,0:T(8,128)} %code_in.1, s32[1,256]{1,0:T(1,128)} %bitcast.9, bf16[256,256]{1,0:T(8,128)(2,1)} %constant.2.clone.oper_in), custom_call_target="tpu_custom_call" | custom-call | tf_op jit(solution)/shard_map/shooting/pallas_call | solution.py:444
  23.5 0.7 %copy.10 = f32[1,3,64,256]{3,2,1,0:T(8,128)} copy(f32[1,3,64,256]{3,2,1,0:T(8,128)S(1)} %bitcast.6) | data formatting | bytes 393216
  24.2 0.7 %copy.11 = f32[1,3,64,256]{3,2,1,0:T(8,128)} copy(f32[1,3,64,256]{3,2,1,0:T(8,128)S(1)} %bitcast.5) | data formatting | bytes 393216

commit v3 on v2

--- a/solution.py
+++ b/solution.py
@@ -100,6 +100,7 @@
     edge_sources,
     halo,
     follow,
+    ready,
     input_sem,
     list_send,
     list_recv,
@@ -117,7 +118,7 @@
     ahead = lax.rem(seg + 1, segs)
     behind = lax.rem(seg + segs - 1, segs)
     barrier = pltpu.get_barrier_semaphore()
-    for target in ({"elem": left}, {"elem": right}, {"seg": ahead}):
+    for target in ({"elem": left}, {"seg": ahead}):
         pl.semaphore_signal(
             barrier, inc=1, device_id=target, device_id_type=pl.DeviceIdType.MESH
         )
@@ -174,12 +175,14 @@
             device_id_type=pl.DeviceIdType.MESH,
         )
 
-    pl.semaphore_wait(barrier, 3)
+    pl.semaphore_wait(barrier, 2)
+    pl.semaphore_signal(
+        ready, inc=1, device_id={"elem": right}, device_id_type=pl.DeviceIdType.MESH
+    )
     for index in range(3):
-        for block in range(2):
-            list_copy(index, block).start()
-    for block in range(2):
-        halo_copy(0, block).start()
+        list_copy(index, 1).start()
+    halo_copy(0, 1).start()
+    follow_copy(0).start()
 
     lane_low = lax.broadcasted_iota(jnp.int32, (NODES, LANES), 1) < HALO
     pack_low = lax.broadcasted_iota(jnp.int32, (96, LANES), 1) < HALO
@@ -268,14 +271,21 @@
 
     for load in loads[5:7]:
         load.wait()
-    for block in range(2):
+
+    def pack_base(block):
         packed = base[block].reshape(COMP * NODES, LANES)
         upper, lower = packed[0:96], pltpu.roll(packed[96:192], HALO, 1)
         base_pack[block] = (
             jnp.where(pack_low, upper, lower) if block == 0 else jnp.where(pack_low, lower, upper)
         )
         base_copy(block).start()
-    follow_copy(0).start()
+
+    pack_base(1)
+    pl.semaphore_wait(ready, 1)
+    for index in range(3):
+        list_copy(index, 0).start()
+    halo_copy(0, 0).start()
+    pack_base(0)
     for block in range(2):
         own_lists(block)
 
@@ -469,6 +479,7 @@
             pltpu.VMEM((2 * COMP * NODES, 3 * LANES), jnp.bfloat16),
             pltpu.VMEM((2, 2, COMP, NODES, LANES), jnp.float32),
             pltpu.VMEM((2, COMP, NODES, SHARD), jnp.float32),
+            pltpu.SemaphoreType.REGULAR,
             pltpu.SemaphoreType.DMA((8,)),
             pltpu.SemaphoreType.DMA((3, 2)),
             pltpu.SemaphoreType.DMA((3, 2)),

time: 25 us -> 25.9 us (1.036)
  the two profiles are of different devices: /device:TPU:24 before, /device:TPU:2 now
where the time goes in v3:
time: 25.9 us; the launch traced here: 25.8 us
  Pallas kernels  23.8 us (92%)
  local copies, waits for them, and re-layouts  1.36 us (5%)
  between operations  0.64 us (2%)
    pallas_call x1, Pallas kernels, on_device(): pl.pallas_call(functools.partial(kernel, lax.axis_size('seg'), lax.axis_s...  23.8 us
    unnamed x2, local copies, waits for them, and re-layouts  1.36 us

profile of v3, /device:TPU:2, one launch (start us, length us, event | category | flops | bytes accessed | tf_op | source)
XLA Modules:
  0.0 25.8 jit_solution(13038721417689915937)
XLA Ops:
  0.6 23.8 %shooting.1 = (f32[3,64,256]{2,1,0:T(8,128)S(1)}, f32[3,64,256]{2,1,0:T(8,128)S(1)}) custom-call(f32[3,64,256]{2,1,0:T(8,128)} %bitcast.7, f32[3,64,256]{2,1,0:T(8,128)} %bitcast.8, s32[6,256]{1,0:T(8,128)} %near_in.1, s32[6,256]{1,0:T(8,128)} %code_in.1, s32[1,256]{1,0:T(1,128)} %bitcast.9, bf16[256,256]{1,0:T(8,128)(2,1)} %constant.2.clone.oper_in), custom_call_target="tpu_custom_call" | custom-call | tf_op jit(solution)/shard_map/shooting/pallas_call | solution.py:454
  24.4 0.7 %copy.10 = f32[1,3,64,256]{3,2,1,0:T(8,128)} copy(f32[1,3,64,256]{3,2,1,0:T(8,128)S(1)} %bitcast.6) | data formatting | bytes 393216
  25.1 0.7 %copy.11 = f32[1,3,64,256]{3,2,1,0:T(8,128)} copy(f32[1,3,64,256]{3,2,1,0:T(8,128)S(1)} %bitcast.5) | data formatting | bytes 393216

commit v4 on v3

--- a/solution.py
+++ b/solution.py
@@ -182,7 +182,6 @@
     for index in range(3):
         list_copy(index, 1).start()
     halo_copy(0, 1).start()
-    follow_copy(0).start()
 
     lane_low = lax.broadcasted_iota(jnp.int32, (NODES, LANES), 1) < HALO
     pack_low = lax.broadcasted_iota(jnp.int32, (96, LANES), 1) < HALO
@@ -281,6 +280,7 @@
         base_copy(block).start()
 
     pack_base(1)
+    follow_copy(0).start()
     pl.semaphore_wait(ready, 1)
     for index in range(3):
         list_copy(index, 0).start()

time: 25.9 us -> 25.9 us (level)
  no operation moved by 1% of the time
where the time goes in v4:
time: 25.9 us; the launch traced here: 25.8 us
  Pallas kernels  23.8 us (92%)
  local copies, waits for them, and re-layouts  1.36 us (5%)
  between operations  0.64 us (2%)
    pallas_call x1, Pallas kernels, on_device(): pl.pallas_call(functools.partial(kernel, lax.axis_size('seg'), lax.axis_s...  23.8 us
    unnamed x2, local copies, waits for them, and re-layouts  1.36 us

profile of v4, /device:TPU:2, one launch (start us, length us, event | category | flops | bytes accessed | tf_op | source)
XLA Modules:
  0.0 25.8 jit_solution(9392192435514496052)
XLA Ops:
  0.6 23.8 %shooting.1 = (f32[3,64,256]{2,1,0:T(8,128)S(1)}, f32[3,64,256]{2,1,0:T(8,128)S(1)}) custom-call(f32[3,64,256]{2,1,0:T(8,128)} %bitcast.7, f32[3,64,256]{2,1,0:T(8,128)} %bitcast.8, s32[6,256]{1,0:T(8,128)} %near_in.1, s32[6,256]{1,0:T(8,128)} %code_in.1, s32[1,256]{1,0:T(1,128)} %bitcast.9, bf16[256,256]{1,0:T(8,128)(2,1)} %constant.2.clone.oper_in), custom_call_target="tpu_custom_call" | custom-call | tf_op jit(solution)/shard_map/shooting/pallas_call | solution.py:454
  24.4 0.7 %copy.10 = f32[1,3,64,256]{3,2,1,0:T(8,128)} copy(f32[1,3,64,256]{3,2,1,0:T(8,128)S(1)} %bitcast.6) | data formatting | bytes 393216
  25.1 0.7 %copy.11 = f32[1,3,64,256]{3,2,1,0:T(8,128)} copy(f32[1,3,64,256]{3,2,1,0:T(8,128)S(1)} %bitcast.5) | data formatting | bytes 393216

commit v5 on v2

--- a/solution.py
+++ b/solution.py
@@ -161,15 +161,16 @@
         source = (probe_in, first_ref)[image].at[:, :, block_lanes[block]]
         return across(source, halo.at[image], halo_send.at[image], halo_recv.at[image], block)
 
-    def follow_copy(image):
-        return arrival(image, (probe_in, first_ref)[image])
-
-    def arrival(image, source=first_ref):
+    def follow_copy(image, block):
+        return arrival(image, block, (probe_in, first_ref)[image])
+
+    def arrival(image, block, source=first_ref):
+        lanes = block_lanes[block]
         return pltpu.make_async_remote_copy(
-            src_ref=source,
-            dst_ref=follow.at[image],
-            send_sem=follow_send.at[image],
-            recv_sem=follow_recv.at[image],
+            src_ref=source.at[:, :, lanes],
+            dst_ref=follow.at[image, :, :, lanes],
+            send_sem=follow_send.at[image, block],
+            recv_sem=follow_recv.at[image, block],
             device_id={"seg": behind},
             device_id_type=pl.DeviceIdType.MESH,
         )
@@ -275,7 +276,8 @@
             jnp.where(pack_low, upper, lower) if block == 0 else jnp.where(pack_low, lower, upper)
         )
         base_copy(block).start()
-    follow_copy(0).start()
+    for block in (1, 0):
+        follow_copy(0, block).start()
     for block in range(2):
         own_lists(block)
 
@@ -412,18 +414,16 @@
             own_terms(block)
         sources[0, :, LANES:SHARD] = pieces_of(blend(block_field(1), block_field(EDGE)))
         sources[1, :, LANES:SHARD] = pieces_of(blend(block_field(EDGE), block_field(0)))
-        for block in range(2):
+        for block in (1, 0):
             own_flux(block)
-        arrival(image).wait_recv()
-        for block in range(2):
+            arrival(image, block).wait_recv()
             lanes = block_lanes[block]
             value = state[block] + TIME_STEP * acc[block] - follow[image, :, :, lanes]
             (first_ref, second_ref)[image][:, :, lanes] = value
             if image == 0:
                 state[block] = value
                 halo_copy(1, block).start()
-        if image == 0:
-            follow_copy(1).start()
+                follow_copy(1, block).start()
 
     for image in range(2):
         one_image(image)
@@ -434,7 +434,8 @@
         for image in range(2):
             halo_copy(image, block).wait_send()
     for image in range(2):
-        follow_copy(image).wait_send()
+        for block in range(2):
+            follow_copy(image, block).wait_send()
 
 
 def on_device(base_flow, probe_field, neighbours, face_codes, face_counts):
@@ -476,8 +477,8 @@
             pltpu.SemaphoreType.DMA((2,)),
             pltpu.SemaphoreType.DMA((2, 2)),
             pltpu.SemaphoreType.DMA((2, 2)),
-            pltpu.SemaphoreType.DMA((2,)),
-            pltpu.SemaphoreType.DMA((2,)),
+            pltpu.SemaphoreType.DMA((2, 2)),
+            pltpu.SemaphoreType.DMA((2, 2)),
         ],
         compiler_params=pltpu.CompilerParams(
             collective_id=0, has_side_effects=True, vmem_limit_bytes=40 * 1024 * 1024

time: 25 us -> 23.1 us (0.924)
  Pallas kernels: 22.9 us -> 21 us
    pallas_call x1, Pallas kernels: 22.9 us -> 21 us  [on_device(): pl.pallas_call(functools.partial(kernel, lax.axis_size('seg'), lax.axis_s...]
where the time goes in v5:
time: 23.1 us; the launch traced here: 23 us
  Pallas kernels  21 us (91%)
  local copies, waits for them, and re-layouts  1.36 us (6%)
  between operations  0.64 us (3%)
    pallas_call x1, Pallas kernels, on_device(): pl.pallas_call(functools.partial(kernel, lax.axis_size('seg'), lax.axis_s...  21 us
    unnamed x2, local copies, waits for them, and re-layouts  1.36 us

profile of v5, /device:TPU:24, one launch (start us, length us, event | category | flops | bytes accessed | tf_op | source)
XLA Modules:
  0.0 23.0 jit_solution(16781671203828550961)
XLA Ops:
  0.6 21.0 %shooting.1 = (f32[3,64,256]{2,1,0:T(8,128)S(1)}, f32[3,64,256]{2,1,0:T(8,128)S(1)}) custom-call(f32[3,64,256]{2,1,0:T(8,128)} %bitcast.7, f32[3,64,256]{2,1,0:T(8,128)} %bitcast.8, s32[6,256]{1,0:T(8,128)} %near_in.1, s32[6,256]{1,0:T(8,128)} %code_in.1, s32[1,256]{1,0:T(1,128)} %bitcast.9, bf16[256,256]{1,0:T(8,128)(2,1)} %constant.2.clone.oper_in), custom_call_target="tpu_custom_call" | custom-call | tf_op jit(solution)/shard_map/shooting/pallas_call | solution.py:445
  21.6 0.7 %copy.10 = f32[1,3,64,256]{3,2,1,0:T(8,128)} copy(f32[1,3,64,256]{3,2,1,0:T(8,128)S(1)} %bitcast.6) | data formatting | bytes 393216
  22.3 0.7 %copy.11 = f32[1,3,64,256]{3,2,1,0:T(8,128)} copy(f32[1,3,64,256]{3,2,1,0:T(8,128)S(1)} %bitcast.5) | data formatting | bytes 393216

commit v6 on v5

--- a/solution.py
+++ b/solution.py
@@ -378,21 +378,20 @@
                     list_copy(index, block).wait_recv()
             edge_lists()
 
-        for side in range(2):
+        def halo_field(side):
+            return lambda comp: halo[image, side, comp]
+
+        for side in (1, 0):
             across(
                 state.at[side], halo.at[image], halo_send.at[image], halo_recv.at[image], 1 - side
             ).wait_recv()
-
-        def halo_field(side):
-            return lambda comp: halo[image, side, comp]
-
-        sources[0, :, LANES:SHARD] = pieces_of(blend(block_field(1), halo_field(0)))
-        sources[1, :, LANES:SHARD] = pieces_of(blend(halo_field(1), block_field(0)))
-        for side in range(2):
+            low, high = block_field(1), halo_field(0)
+            if side == 1:
+                low, high = halo_field(1), block_field(0)
+            sources[side, :, LANES:SHARD] = pieces_of(blend(low, high))
             lanes = slice((side + 1) * LANES, (side + 2) * LANES)
             edge_sources[:, lanes] = pieces_of([halo[image, side, comp] for comp in range(COMP)])
-        for block in range(2):
-            own_flux(block)
+            own_flux(side)
         edge = blend(halo_field(1), halo_field(0))
         for comp in range(COMP):
             state[EDGE, comp] = edge[comp]

time: 23.1 us -> 23.1 us (level)
  no operation moved by 1% of the time
where the time goes in v6:
time: 23.1 us; the launch traced here: 23 us
  Pallas kernels  21 us (91%)
  local copies, waits for them, and re-layouts  1.36 us (6%)
  between operations  0.64 us (3%)
    pallas_call x1, Pallas kernels, on_device(): pl.pallas_call(functools.partial(kernel, lax.axis_size('seg'), lax.axis_s...  21 us
    unnamed x2, local copies, waits for them, and re-layouts  1.36 us

profile of v6, /device:TPU:24, one launch (start us, length us, event | category | flops | bytes accessed | tf_op | source)
XLA Modules:
  0.0 23.0 jit_solution(11248178340472559252)
XLA Ops:
  0.6 21.0 %shooting.1 = (f32[3,64,256]{2,1,0:T(8,128)S(1)}, f32[3,64,256]{2,1,0:T(8,128)S(1)}) custom-call(f32[3,64,256]{2,1,0:T(8,128)} %bitcast.7, f32[3,64,256]{2,1,0:T(8,128)} %bitcast.8, s32[6,256]{1,0:T(8,128)} %near_in.1, s32[6,256]{1,0:T(8,128)} %code_in.1, s32[1,256]{1,0:T(1,128)} %bitcast.9, bf16[256,256]{1,0:T(8,128)(2,1)} %constant.2.clone.oper_in), custom_call_target="tpu_custom_call" | custom-call | tf_op jit(solution)/shard_map/shooting/pallas_call | solution.py:444
  21.6 0.7 %copy.10 = f32[1,3,64,256]{3,2,1,0:T(8,128)} copy(f32[1,3,64,256]{3,2,1,0:T(8,128)S(1)} %bitcast.6) | data formatting | bytes 393216
  22.3 0.7 %copy.11 = f32[1,3,64,256]{3,2,1,0:T(8,128)} copy(f32[1,3,64,256]{3,2,1,0:T(8,128)S(1)} %bitcast.5) | data formatting | bytes 393216
